TPU v7x, 32 devices: a whole 2x2x4 slice. The times are simulated.
32 devices in a mesh: slab: 8 (over y, x, core), probe: 4 (over z).
Axes of the slice: x: 2, y: 2, z: 4, core: 2. Of those that a mesh axis runs over, the one named last changes fastest.
Arguments:
- probe_fields: bfloat16 [256, 32, 8192], P('probe', 'slab'), may hold values from -6 to 6
- sensor_rows: int32 [4096], replicated, may hold values from 0 to 30, as said below
- sensor_cols: int32 [4096], replicated, may hold values from 0 to 8190
- row_frac: float32 [4096], replicated, may hold values from 0 to 1
- col_frac: float32 [4096], replicated, may hold values from 0 to 1
- sensor_weights: float32 [4096], replicated, may hold values from 0.05 to 1
- owner_order: int32 [4096], replicated, may hold values from 0 to 4095, as said below
Outputs:
- adjoint_sources: bfloat16 [256, 32, 8192], P('probe', 'slab')
- observed: float32 [256, 4096], P('probe', 'slab')
- trace_mean: float32 [], replicated
Inputs may be any that keep to these rules, and one draw needn't show every extreme that they name: `sensor_rows`: rows run from 0 to 30. The sensors whose row lies in one slab of 4 rows number at most 2048, and some slab holds exactly 2048. `owner_order`: A permutation. The 4096 // 8 slots of one owner name at most 256 sensors whose row lies in any one slab, and every owner reaches 256 for some slab.
All inputs are finite; a program needn't handle non-finite values.
Results may differ from a plain program's by a relative error of at most 0.0068.
Values sent between devices are 32-bit elements; how exact they have to be, the bound alone decides.
A program may use at most 64 MiB of HBM per device.

v0:
```python
import jax
import jax.numpy as jnp
from jax import lax
from jax.sharding import PartitionSpec as P


def column_table(columns, fractions, start, count, across):
    low_value = (1.0 - fractions).astype(jnp.bfloat16)
    high_value = fractions.astype(jnp.bfloat16)
    zero_value = jnp.zeros((), jnp.bfloat16)
    if across:
        cells = start + lax.broadcasted_iota(jnp.int32, (columns.shape[0], count), 1)
        where_col = columns[:, None]
        low_b = low_value[:, None]
        high_b = high_value[:, None]
    else:
        cells = start + lax.broadcasted_iota(jnp.int32, (count, columns.shape[0]), 0)
        where_col = columns[None, :]
        low_b = low_value[None, :]
        high_b = high_value[None, :]
    return jnp.where(
        cells == where_col, low_b, jnp.where(cells == where_col + 1, high_b, zero_value)
    )


def adjoint_grid(sources, columns, fractions, width):
    column_block = min(1024, width)

    def adjoint_block(number, result):
        begin = number * column_block
        table = column_table(columns, fractions, begin, column_block, True)
        piece = jnp.dot(sources, table, preferred_element_type=jnp.float32)
        return lax.dynamic_update_slice_in_dim(result, piece.astype(jnp.bfloat16), begin, 1)

    return lax.fori_loop(
        0, width // column_block, adjoint_block, jnp.zeros((sources.shape[0], width), jnp.bfloat16)
    )


def body(probe_fields, sensor_rows, sensor_cols, row_frac, col_frac, sensor_weights, owner_order):
    probe_count, row_count, width = probe_fields.shape
    sensor_count = sensor_rows.shape[0]
    depth = probe_count * row_count
    owned_rows = sensor_rows[owner_order]
    owned_cols = sensor_cols[owner_order]
    owned_rowfrac = row_frac[owner_order]
    owned_colfrac = col_frac[owner_order]
    owned_weights = sensor_weights[owner_order]
    slab_index = lax.axis_index("slab")
    first_row = slab_index * row_count
    slab_count = lax.axis_size("slab")
    own_count = sensor_count // slab_count
    own_begin = slab_index * own_count
    total_count = probe_count * lax.axis_size("probe") * sensor_count
    local_rows = first_row + lax.broadcasted_iota(jnp.int32, (row_count, sensor_count), 0)
    row_weights = jnp.where(local_rows == owned_rows[None, :], 1.0 - owned_rowfrac[None, :], 0.0)
    row_weights = row_weights + jnp.where(
        local_rows == owned_rows[None, :] + 1, owned_rowfrac[None, :], 0.0
    )
    flat_fields = probe_fields.reshape(depth, width)
    sensor_block = min(512, sensor_count)

    def forward_block(number, partial_value):
        begin = number * sensor_block
        cols_block = lax.dynamic_slice_in_dim(owned_cols, begin, sensor_block)
        frac_block = lax.dynamic_slice_in_dim(owned_colfrac, begin, sensor_block)
        table = column_table(cols_block, frac_block, 0, width, False)
        along = jnp.dot(flat_fields, table, preferred_element_type=jnp.float32)
        along = along.reshape(probe_count, row_count, sensor_block)
        weights_block = lax.dynamic_slice_in_dim(row_weights, begin, sensor_block, 1)
        summed = jnp.sum(along * weights_block[None, :, :], axis=1)
        return lax.dynamic_update_slice_in_dim(partial_value, summed, begin, 1)

    partial_value = lax.fori_loop(
        0,
        sensor_count // sensor_block,
        forward_block,
        jnp.zeros((probe_count, sensor_count), jnp.float32),
    )
    observed_all = lax.psum(partial_value, "slab")
    spread = observed_all * owned_weights[None, :]
    observed = lax.dynamic_slice_in_dim(observed_all, own_begin, own_count, 1)
    total = lax.psum(jnp.sum(spread * observed_all), "probe")
    sources = (spread[:, None, :] * row_weights[None, :, :]).astype(jnp.bfloat16)
    sources = sources.reshape(depth, sensor_count)
    result = adjoint_grid(sources, owned_cols, owned_colfrac, width)
    trace_mean = total / total_count
    adjoint_sources = result.reshape(probe_count, row_count, width)
    return (adjoint_sources, observed, trace_mean)


def solution(mesh):
    placed = (P("probe", "slab", None), P(), P(), P(), P(), P(), P())
    return jax.shard_map(
        body,
        mesh=mesh,
        in_specs=placed,
        out_specs=(P("probe", "slab", None), P("probe", "slab"), P()),
        check_vma=False,
    )
```

profile of v0, /device:TPU:4, one launch (start us, length us, event | category | flops | bytes accessed | tf_op | source)
XLA Modules:
  0.0 339.4 jit_solution(7330105673134998038)
XLA Ops:
  8.0 23.0 %gather_fusion.1 = f32[4096]{0:T(1024)S(1)} fusion(f32[4096]{0:T(1024)S(1)} %copy-done, s32[4096]{0:T(1024)S(1)} %fusion.23), kind=kCustom, calls=%fused_computation.1 | custom fusion | bytes 49152 | tf_op jit(solution)/shard_map/gather | solution.py:47
  31.0 23.0 %gather_fusion.3 = f32[4096]{0:T(1024)S(1)} fusion(f32[4096]{0:T(1024)S(1)} %copy-done.1, s32[4096]{0:T(1024)S(1)} %fusion.23), kind=kCustom, calls=%fused_computation.3 | custom fusion | bytes 49152 | tf_op jit(solution)/shard_map/gather | solution.py:46
  54.1 23.0 %gather_fusion.2 = s32[4096]{0:T(1024)S(1)} fusion(s32[4096]{0:T(1024)S(1)} %copy-done.2, s32[4096]{0:T(1024)S(1)} %fusion.23), kind=kCustom, calls=%fused_computation.2 | custom fusion | bytes 49152 | tf_op jit(solution)/shard_map/gather | solution.py:44
  77.2 23.0 %gather_fusion = s32[4096]{0:T(1024)S(1)} fusion(s32[4096]{0:T(1024)S(1)} %copy-done.3, s32[4096]{0:T(1024)S(1)} %fusion.23), kind=kCustom, calls=%fused_computation | custom fusion | bytes 49152 | tf_op jit(solution)/shard_map/gather | solution.py:45
  100.2 6.9 %reshape.146 = bf16[256,8192]{1,0:T(8,128)(2,1)} reshape(bf16[64,4,8192]{2,1,0:T(4,128)(2,1)} %param.11) | data formatting | bytes 8388608 | tf_op jit(solution)/shard_map/reshape | solution.py:60
  107.3 48.5 %while.28 = (s32[]{:T(128)}, f32[64,4096]{1,0:T(8,128)S(1)}, s32[4096]{0:T(1024)S(1)}, f32[4096]{0:T(1024)S(1)}, bf16[256,8192]{1,0:T(8,128)(2,1)}, /*index=5*/f...) while((s32[]{:T(128)}, f32[64,4096]{1,0:T(8,128)S(1)}, s32[4096]{0:T(1024)S(1)}, ...), condition=%wide.region_2.3_spmd, body=%wide.region_0.2_spmd.sunk | while | flops 2164491776 | bytes 6726823 | solution.py:74
  107.5 5.3 %fusion.33 = f32[256,512]{1,0:T(8,128)S(1)} fusion(bf16[256,8192]{1,0:T(8,128)(2,1)} %get-tuple-element.389, s32[512]{0:T(512)S(1)} %get-tuple-element.356, s32[512]{0:T(512)S(1)} %get-tuple-element.357, bf16[512]{0:T(512)(128)(2,1)S(1)} %dynamic_slice.38, bf16[512]{0:T(512)(128)(2,1)S(1)} %subtract_convert_fusion.4), kind=kOutput, calls=%fused_computation.14.clone.1 | convolution fusion | flops 2164260864 | bytes 4724736 | tf_op jit(solution)/shard_map/while/body/eval_jaxpr/dot_general | solution.py:68
  119.7 5.3 %fusion.33 = f32[256,512]{1,0:T(8,128)S(1)} fusion(bf16[256,8192]{1,0:T(8,128)(2,1)} %get-tuple-element.389, s32[512]{0:T(512)S(1)} %get-tuple-element.356, s32[512]{0:T(512)S(1)} %get-tuple-element.357, bf16[512]{0:T(512)(128)(2,1)S(1)} %dynamic_slice.38, bf16[512]{0:T(512)(128)(2,1)S(1)} %subtract_convert_fusion.4), kind=kOutput, calls=%fused_computation.14.clone.1 | convolution fusion | flops 2164260864 | bytes 4724736 | tf_op jit(solution)/shard_map/while/body/eval_jaxpr/dot_general | solution.py:68
  125.7 5.3 %fusion.33 = f32[256,512]{1,0:T(8,128)S(1)} fusion(bf16[256,8192]{1,0:T(8,128)(2,1)} %get-tuple-element.389, s32[512]{0:T(512)S(1)} %get-tuple-element.356, s32[512]{0:T(512)S(1)} %get-tuple-element.357, bf16[512]{0:T(512)(128)(2,1)S(1)} %dynamic_slice.38, bf16[512]{0:T(512)(128)(2,1)S(1)} %subtract_convert_fusion.4), kind=kOutput, calls=%fused_computation.14.clone.1 | convolution fusion | flops 2164260864 | bytes 4724736 | tf_op jit(solution)/shard_map/while/body/eval_jaxpr/dot_general | solution.py:68
  137.9 5.3 %fusion.33 = f32[256,512]{1,0:T(8,128)S(1)} fusion(bf16[256,8192]{1,0:T(8,128)(2,1)} %get-tuple-element.389, s32[512]{0:T(512)S(1)} %get-tuple-element.356, s32[512]{0:T(512)S(1)} %get-tuple-element.357, bf16[512]{0:T(512)(128)(2,1)S(1)} %dynamic_slice.38, bf16[512]{0:T(512)(128)(2,1)S(1)} %subtract_convert_fusion.4), kind=kOutput, calls=%fused_computation.14.clone.1 | convolution fusion | flops 2164260864 | bytes 4724736 | tf_op jit(solution)/shard_map/while/body/eval_jaxpr/dot_general | solution.py:68
  143.9 5.3 %fusion.33 = f32[256,512]{1,0:T(8,128)S(1)} fusion(bf16[256,8192]{1,0:T(8,128)(2,1)} %get-tuple-element.389, s32[512]{0:T(512)S(1)} %get-tuple-element.356, s32[512]{0:T(512)S(1)} %get-tuple-element.357, bf16[512]{0:T(512)(128)(2,1)S(1)} %dynamic_slice.38, bf16[512]{0:T(512)(128)(2,1)S(1)} %subtract_convert_fusion.4), kind=kOutput, calls=%fused_computation.14.clone.1 | convolution fusion | flops 2164260864 | bytes 4724736 | tf_op jit(solution)/shard_map/while/body/eval_jaxpr/dot_general | solution.py:68
  156.9 23.0 %gather_fusion.4 = f32[4096]{0:T(1024)S(1)} fusion(f32[4096]{0:T(1024)S(1)} %copy-done.4, s32[4096]{0:T(1024)S(1)} %fusion.23), kind=kCustom, calls=%fused_computation.4 | custom fusion | bytes 49152 | tf_op jit(solution)/shard_map/gather | solution.py:48
  179.9 34.1 %all-reduce.2.cloned.1.call-done = f32[64,4096]{1,0:T(8,128)} async-done(((f32[64,4096]{1,0:T(8,128)}), f32[64,4096]{1,0:T(8,128)}) %all-reduce.2.cloned.1.call-update) | async-done | bytes 1048592 | tf_op jit(solution)/shard_map/psum | solution.py:80
  216.1 12.5 %psum.15 = f32[]{:T(128)} all-reduce(f32[]{:T(128)} %get-tuple-element.279), channel_id=1, replica_groups=mesh['slab'=8,'probe'=4] {'probe'}, use_global_device_ids=true, to_apply=%region_7.8 | all-reduce | flops 1 | bytes 8 | tf_op jit(solution)/shard_map/psum | solution.py:83
  231.0 91.1 %while.29 = (s32[]{:T(128)}, bf16[256,8192]{1,0:T(8,128)(2,1)}, s32[4096]{0:T(1024)S(1)}, f32[4096]{0:T(1024)S(1)}, bf16[4096,1]{0,1:T(2,128)(2,1)S(1)}, /*index...) while((s32[]{:T(128)}, bf16[256,8192]{1,0:T(8,128)(2,1)}, ...), condition=%wide.region_5.6_spmd.clone, body=%wide.region_4.5_spmd.clone.sunk | while | flops 2166633472 | bytes 12255405 | solution.py:35
  234.2 7.0 %fusion.35 = bf16[256,1024]{0,1:T(8,128)(2,1)S(1)} fusion(bf16[256,4096]{1,0:T(8,128)(2,1)} %convert_element_type.94, s32[1024]{0:T(1024)S(1)} %iota_add_fusion.3, s32[4096]{0:T(1024)S(1)} %broadcast_add_fusion.6, s32[4096]{0:T(1024)S(1)} %get-tuple-element.421, bf16[4096]{0:T(1024)(128)(2,1)S(1)} %reduce.2, ...), kind=kOutput, calls=%fused_computation.33.clone.1 | convolution fusion | flops 2164523008 | bytes 2674688 | tf_op jit(solution)/shard_map/while/body/eval_jaxpr/dot_general | solution.py:32
  245.7 7.0 %fusion.35 = bf16[256,1024]{0,1:T(8,128)(2,1)S(1)} fusion(bf16[256,4096]{1,0:T(8,128)(2,1)} %convert_element_type.94, s32[1024]{0:T(1024)S(1)} %iota_add_fusion.3, s32[4096]{0:T(1024)S(1)} %broadcast_add_fusion.6, s32[4096]{0:T(1024)S(1)} %get-tuple-element.421, bf16[4096]{0:T(1024)(128)(2,1)S(1)} %reduce.2, ...), kind=kOutput, calls=%fused_computation.33.clone.1 | convolution fusion | flops 2164523008 | bytes 2674688 | tf_op jit(solution)/shard_map/while/body/eval_jaxpr/dot_general | solution.py:32
  257.0 7.0 %fusion.35 = bf16[256,1024]{0,1:T(8,128)(2,1)S(1)} fusion(bf16[256,4096]{1,0:T(8,128)(2,1)} %convert_element_type.94, s32[1024]{0:T(1024)S(1)} %iota_add_fusion.3, s32[4096]{0:T(1024)S(1)} %broadcast_add_fusion.6, s32[4096]{0:T(1024)S(1)} %get-tuple-element.421, bf16[4096]{0:T(1024)(128)(2,1)S(1)} %reduce.2, ...), kind=kOutput, calls=%fused_computation.33.clone.1 | convolution fusion | flops 2164523008 | bytes 2674688 | tf_op jit(solution)/shard_map/while/body/eval_jaxpr/dot_general | solution.py:32
  268.4 7.0 %fusion.35 = bf16[256,1024]{0,1:T(8,128)(2,1)S(1)} fusion(bf16[256,4096]{1,0:T(8,128)(2,1)} %convert_element_type.94, s32[1024]{0:T(1024)S(1)} %iota_add_fusion.3, s32[4096]{0:T(1024)S(1)} %broadcast_add_fusion.6, s32[4096]{0:T(1024)S(1)} %get-tuple-element.421, bf16[4096]{0:T(1024)(128)(2,1)S(1)} %reduce.2, ...), kind=kOutput, calls=%fused_computation.33.clone.1 | convolution fusion | flops 2164523008 | bytes 2674688 | tf_op jit(solution)/shard_map/while/body/eval_jaxpr/dot_general | solution.py:32
  279.8 7.0 %fusion.35 = bf16[256,1024]{0,1:T(8,128)(2,1)S(1)} fusion(bf16[256,4096]{1,0:T(8,128)(2,1)} %convert_element_type.94, s32[1024]{0:T(1024)S(1)} %iota_add_fusion.3, s32[4096]{0:T(1024)S(1)} %broadcast_add_fusion.6, s32[4096]{0:T(1024)S(1)} %get-tuple-element.421, bf16[4096]{0:T(1024)(128)(2,1)S(1)} %reduce.2, ...), kind=kOutput, calls=%fused_computation.33.clone.1 | convolution fusion | flops 2164523008 | bytes 2674688 | tf_op jit(solution)/shard_map/while/body/eval_jaxpr/dot_general | solution.py:32
  291.2 7.0 %fusion.35 = bf16[256,1024]{0,1:T(8,128)(2,1)S(1)} fusion(bf16[256,4096]{1,0:T(8,128)(2,1)} %convert_element_type.94, s32[1024]{0:T(1024)S(1)} %iota_add_fusion.3, s32[4096]{0:T(1024)S(1)} %broadcast_add_fusion.6, s32[4096]{0:T(1024)S(1)} %get-tuple-element.421, bf16[4096]{0:T(1024)(128)(2,1)S(1)} %reduce.2, ...), kind=kOutput, calls=%fused_computation.33.clone.1 | convolution fusion | flops 2164523008 | bytes 2674688 | tf_op jit(solution)/shard_map/while/body/eval_jaxpr/dot_general | solution.py:32
  302.6 7.0 %fusion.35 = bf16[256,1024]{0,1:T(8,128)(2,1)S(1)} fusion(bf16[256,4096]{1,0:T(8,128)(2,1)} %convert_element_type.94, s32[1024]{0:T(1024)S(1)} %iota_add_fusion.3, s32[4096]{0:T(1024)S(1)} %broadcast_add_fusion.6, s32[4096]{0:T(1024)S(1)} %get-tuple-element.421, bf16[4096]{0:T(1024)(128)(2,1)S(1)} %reduce.2, ...), kind=kOutput, calls=%fused_computation.33.clone.1 | convolution fusion | flops 2164523008 | bytes 2674688 | tf_op jit(solution)/shard_map/while/body/eval_jaxpr/dot_general | solution.py:32
  313.9 7.0 %fusion.35 = bf16[256,1024]{0,1:T(8,128)(2,1)S(1)} fusion(bf16[256,4096]{1,0:T(8,128)(2,1)} %convert_element_type.94, s32[1024]{0:T(1024)S(1)} %iota_add_fusion.3, s32[4096]{0:T(1024)S(1)} %broadcast_add_fusion.6, s32[4096]{0:T(1024)S(1)} %get-tuple-element.421, bf16[4096]{0:T(1024)(128)(2,1)S(1)} %reduce.2, ...), kind=kOutput, calls=%fused_computation.33.clone.1 | convolution fusion | flops 2164523008 | bytes 2674688 | tf_op jit(solution)/shard_map/while/body/eval_jaxpr/dot_general | solution.py:32
  322.1 7.2 %reshape.147 = bf16[64,4,8192]{2,1,0:T(4,128)(2,1)} reshape(bf16[256,8192]{1,0:T(8,128)(2,1)} %get-tuple-element.232) | data formatting | bytes 8388608 | tf_op jit(solution)/shard_map/reshape | solution.py:88
  (148 shorter events, 64.3 us)
Async XLA Ops:
  7.2 0.8 copy-start
  7.2 206.8 %all-reduce.2.cloned.1.call-start = ((), (), s32[]{:S(2)}) async-start(), calls=%async_computation | async-start | bytes 2097152 | tf_op jit(solution)/shard_map/psum | solution.py:80
  8.0 23.1 %copy-start.1 = (f32[4096]{0:T(1024)S(1)}, f32[4096]{0:T(1024)}, u32[]{:S(2)}) copy-start(f32[4096]{0:T(1024)} %param.14) | copy-start | bytes 49156
  31.0 23.1 %copy-start.2 = (s32[4096]{0:T(1024)S(1)}, s32[4096]{0:T(1024)}, u32[]{:S(2)}) copy-start(s32[4096]{0:T(1024)} %param.12) | copy-start | bytes 49156
  54.1 23.1 %copy-start.3 = (s32[4096]{0:T(1024)S(1)}, s32[4096]{0:T(1024)}, u32[]{:S(2)}) copy-start(s32[4096]{0:T(1024)} %param.13) | copy-start | bytes 49156
  155.8 1.0 copy-start.5
  155.8 1.0 copy-start.4
Sparse Core Ops, SparseCore 0:
  156.9 56.9 all-reduce.1
where the time goes:
time: 343 us; the launch traced here: 339 us
  local copies, waits for them, and re-layouts  161 us (47%)
  matrix products  98.4 us (29%)
  waiting for transfers between devices  34.1 us (10%)
  other arithmetic  16.7 us (5%)
  between operations  16 us (5%)
  blocking collectives  12.5 us (4%)
    dot_general x8, matrix products, adjoint_block(): piece = jnp.dot(sources, table, preferred_element_type=jnp.float32)  56.2 us
    dot_general x8, matrix products, forward_block(): along = jnp.dot(flat_fields, table, preferred_element_type=jnp.float32)  42.2 us
    psum x1, waiting for transfers between devices, body(): observed_all = lax.psum(partial_value, 'slab')  34.1 us
    gather x1, local copies, waits for them, and re-layouts, body(): owned_colfrac = col_frac[owner_order]  23 us
    gather x1, local copies, waits for them, and re-layouts, body(): owned_rowfrac = row_frac[owner_order]  23 us
    gather x1, local copies, waits for them, and re-layouts, body(): owned_rows = sensor_rows[owner_order]  23 us
    gather x1, local copies, waits for them, and re-layouts, body(): owned_cols = sensor_cols[owner_order]  23 us
    gather x1, local copies, waits for them, and re-layouts, body(): owned_weights = sensor_weights[owner_order]  23 us
  transfers between devices with their start and end apart: 1, of which 1 were waited for; matrix products, arithmetic and copies ran while one was open for 7% of the time, Pallas kernels for 0%

commit v1 on v0

v1 whole, which is shorter than its diff:
```python
import functools

import jax
import jax.numpy as jnp
from jax import lax
from jax.experimental import pallas as pl
from jax.experimental.pallas import tpu as pltpu
from jax.sharding import PartitionSpec as P

LANES = 128
BLOCK = 256
FIELDS = 11
F32 = jnp.float32
BF16 = jnp.bfloat16
NT = (((1,), (1,)), ((), ()))
VMEM = pltpu.VMEM
SMEM = pltpu.SMEM
LIMIT = pltpu.CompilerParams(vmem_limit_bytes=60 * 1024 * 1024)


def iota(shape, dim):
    return lax.broadcasted_iota(jnp.int32, shape, dim)


def nt_dot(a, b):
    return lax.dot_general(a, b, NT, preferred_element_type=F32)


def plan_kernel(rows, cap_chunks, blocks, first_ref, r_ref, c_ref, rf_ref, cf_ref, w_ref, order_ref, plan_ref, lo_ref, hi_ref):
    lines = r_ref.shape[0]
    sensors = lines * LANES
    step = min(4, lines)
    first = first_ref[0]
    keys_group = 2 * blocks
    keys = 3 * keys_group
    chunks = 3 * cap_chunks

    def wide(x, i):
        return jnp.concatenate([x[i + j : i + j + 1, :] for j in range(step)], axis=1)

    order = order_ref[...]
    slot = iota((lines, LANES), 0) * LANES + iota((lines, LANES), 1)
    found = jnp.zeros((2 * lines, LANES), F32)
    for i in range(0, lines, step):
        target = wide(order, i)
        mine = wide(slot, i)
        here = iota((lines, step * LANES), 0) == (target >> 7)
        stack = jnp.concatenate(
            [jnp.where(here, (mine >> 7).astype(F32), 0.0), jnp.where(here, (mine & 127).astype(F32), 0.0)], axis=0
        ).astype(BF16)
        place = jnp.where(iota((LANES, step * LANES), 0) == (target & 127), 1.0, 0.0).astype(BF16)
        found = found + nt_dot(stack, place)
    slot_hi = found[:lines, :]
    slot_lo = found[lines:, :]

    r = r_ref[...]
    c = c_ref[...]
    rel = r - first + 1
    valid = (rel >= 0) & (rel <= rows)
    group = jnp.where(rel == 0, 0, jnp.where(rel == rows, 2, 1))
    block = c // BLOCK
    inner = c - block * BLOCK
    key = group * keys_group + 2 * block + jnp.where(inner == BLOCK - 1, 1, 0)
    key = jnp.where(valid, key, -1)

    count = jnp.zeros((keys, 1), F32)
    for i in range(lines):
        count = count + jnp.sum(jnp.where(iota((keys, LANES), 0) == key[i : i + 1, :], 1.0, 0.0), axis=1, keepdims=True)
    big = jnp.floor(count * (1.0 / 64.0))
    small = count - 64.0 * big
    ka, kb = iota((keys, keys), 0), iota((keys, keys), 1)
    below = jnp.where((kb < ka) & (kb // keys_group == ka // keys_group), 1.0, 0.0).astype(BF16)
    start = 64.0 * jnp.dot(below, jnp.broadcast_to(big, (keys, LANES)).astype(BF16), preferred_element_type=F32)
    start = start + jnp.dot(below, jnp.broadcast_to(small, (keys, LANES)).astype(BF16), preferred_element_type=F32)
    start = start + ((iota((keys, LANES), 0) // keys_group) * (cap_chunks * LANES)).astype(F32)
    lo_ref[...] = start.astype(jnp.int32)
    hi_ref[...] = (start + count).astype(jnp.int32)

    upper = jnp.where(iota((LANES, LANES), 0) < iota((LANES, LANES), 1), 1.0, 0.0).astype(BF16)
    carry = start[:, :1]
    spots = []
    for i in range(lines):
        hot = jnp.where(iota((keys, LANES), 0) == key[i : i + 1, :], 1.0, 0.0)
        before = jnp.dot(hot.astype(BF16), upper, preferred_element_type=F32)
        spots.append(jnp.sum(hot * (before + carry), axis=0, keepdims=True))
        carry = carry + jnp.sum(hot, axis=1, keepdims=True)
    spot = jnp.concatenate(spots, axis=0).astype(jnp.int32)
    spot = jnp.where(valid, spot, -1)

    rf = rf_ref[...]
    cf = cf_ref[...]
    w = w_ref[...]
    rf_top = rf.astype(BF16).astype(F32)
    w_top = w.astype(BF16).astype(F32)
    values = [
        block.astype(F32),
        inner.astype(F32),
        (1.0 - cf).astype(BF16).astype(F32),
        cf.astype(BF16).astype(F32),
        rf_top,
        rf - rf_top,
        w_top,
        w - w_top,
        rel.astype(F32),
        slot_hi,
        slot_lo,
    ]
    total = jnp.zeros((FIELDS * chunks, LANES), F32)
    for i in range(0, lines, step):
        target = wide(spot, i)
        here = iota((chunks, step * LANES), 0) == (target >> 7)
        stack = jnp.concatenate([jnp.where(here, wide(v, i), 0.0) for v in values], axis=0).astype(BF16)
        place = jnp.where(iota((LANES, step * LANES), 0) == (target & 127), 1.0, 0.0).astype(BF16)
        total = total + nt_dot(stack, place)
    for f in range(FIELDS):
        plan_ref[f] = total[f * chunks : (f + 1) * chunks, :]


def column_table(plan_ref, chunk, number):
    line = pl.ds(chunk, 1)
    column = ((plan_ref[0, line, :] - number.astype(F32)) * BLOCK + plan_ref[1, line, :]).astype(jnp.int32)
    cells = iota((BLOCK, LANES), 0)
    return jnp.where(
        cells == column, plan_ref[2, line, :], jnp.where(cells == column + 1, plan_ref[3, line, :], 0.0)
    ).astype(BF16)


def row_pattern(plan_ref, chunk, rows, depth):
    line = pl.ds(chunk, 1)
    rf = plan_ref[4, line, :] + plan_ref[5, line, :]
    rel = plan_ref[8, line, :].astype(jnp.int32)
    row = iota((depth, LANES), 0) % rows + 1
    return jnp.where(row == rel, 1.0 - rf, jnp.where(row == rel + 1, rf, 0.0))


def group_chunks(hi_ref, group, keys_group, base):
    return (hi_ref[(group + 1) * keys_group - 1] - base + LANES - 1) // LANES


def chunk_range(lo_ref, hi_ref, group, number, keys_group):
    at = group * keys_group + 2 * number
    begin = lo_ref[jnp.maximum(at - 1, group * keys_group)]
    end = hi_ref[at + 1]
    return begin // LANES, jnp.where(end > begin, (end + LANES - 1) // LANES, begin // LANES)


def forward_kernel(cap_chunks, field_ref, plan_ref, lo_ref, hi_ref, value_ref, slots_ref, flat, sums, parts):
    probes, rows, width = field_ref.shape
    depth = probes * rows
    blocks = width // BLOCK
    keys_group = 2 * blocks
    lines = parts.shape[0]
    parts[...] = jnp.zeros_like(parts)
    counts = [group_chunks(hi_ref, g, keys_group, g * cap_chunks * LANES) for g in range(3)]
    for g in range(3):

        @pl.loop(0, counts[g])
        def _(k):
            sums[g * cap_chunks + k] = jnp.zeros((depth, LANES), F32)

    @pl.loop(0, blocks)
    def _(number):
        cols = pl.ds(pl.multiple_of(number * BLOCK, BLOCK), BLOCK)
        flat[...] = field_ref[:, :, cols].astype(F32).reshape(depth, BLOCK).astype(BF16)
        for g in range(3):
            begin, end = chunk_range(lo_ref, hi_ref, g, number, keys_group)

            @pl.loop(begin, end)
            def _(chunk):
                table = column_table(plan_ref, chunk, number)
                sums[chunk] += jnp.dot(flat[...], table, preferred_element_type=F32)

    fold = jnp.where(iota((probes, depth), 1) // rows == iota((probes, depth), 0), 1.0, 0.0).astype(BF16)
    for g in range(3):

        @pl.loop(0, counts[g])
        def _(k):
            chunk = g * cap_chunks + k
            scaled = (sums[chunk] * row_pattern(plan_ref, chunk, rows, depth)).astype(BF16)
            value = jnp.dot(fold, scaled, preferred_element_type=F32)
            value_ref[:, pl.ds(pl.multiple_of(chunk * LANES, LANES), LANES)] = value
            line = pl.ds(chunk, 1)
            high = plan_ref[9, line, :].astype(jnp.int32)
            low = plan_ref[10, line, :].astype(jnp.int32)
            place = jnp.where(iota((LANES, LANES), 0) == low, 1.0, 0.0).astype(BF16)
            stack = jnp.concatenate([jnp.where(high == d, value, 0.0) for d in range(lines)], axis=0).astype(BF16)
            parts[...] += nt_dot(stack, place).reshape(lines, probes, LANES)

    for d in range(lines):
        slots_ref[:, d * LANES : (d + 1) * LANES] = parts[d]


def adjoint_kernel(cap_chunks, value_ref, above_ref, below_ref, plan_ref, lo_ref, hi_ref, out_ref, trace_ref, sources, total, squares):
    probes, rows, width = out_ref.shape
    depth = probes * rows
    blocks = width // BLOCK
    keys_group = 2 * blocks
    squares[...] = jnp.zeros_like(squares)
    spread_out = jnp.where(iota((depth, probes), 0) // rows == iota((depth, probes), 1), 1.0, 0.0).astype(BF16)
    for g in range(3):
        count = group_chunks(hi_ref, g, keys_group, g * cap_chunks * LANES)

        @pl.loop(0, count)
        def _(k):
            chunk = g * cap_chunks + k
            value = value_ref[:, pl.ds(pl.multiple_of(chunk * LANES, LANES), LANES)]
            near = pl.ds(pl.multiple_of(k * LANES, LANES), LANES)
            if g == 0:
                value = value + below_ref[:, near]
            if g == 2:
                value = value + above_ref[:, near]
            line = pl.ds(chunk, 1)
            spread = value * (plan_ref[6, line, :] + plan_ref[7, line, :])
            if g > 0:
                squares[...] += spread * value
            raised = jnp.dot(spread_out, spread.astype(BF16), preferred_element_type=F32)
            sources[chunk] = (raised * row_pattern(plan_ref, chunk, rows, depth)).astype(BF16)

    trace_ref[...] = jnp.sum(squares[...], axis=0, keepdims=True)

    @pl.loop(0, blocks)
    def _(number):
        total[...] = jnp.zeros_like(total)
        for g in range(3):
            begin, end = chunk_range(lo_ref, hi_ref, g, number, keys_group)

            @pl.loop(begin, end)
            def _(chunk):
                total[...] += nt_dot(sources[chunk], column_table(plan_ref, chunk, number))

        cols = pl.ds(pl.multiple_of(number * BLOCK, BLOCK), BLOCK)
        out_ref[:, :, cols] = total[...].reshape(probes, rows, BLOCK).astype(BF16)


def body(slab_count, probe_groups, probe_fields, sensor_rows, sensor_cols, row_frac, col_frac, sensor_weights, owner_order):
    probes, rows, width = probe_fields.shape
    sensors = sensor_rows.shape[0]
    depth = probes * rows
    lines = sensors // LANES
    blocks = width // BLOCK
    keys = 6 * blocks
    most = min(sensors, 4 * sensors // slab_count)
    cap_chunks = -(-most // (8 * LANES)) * 8
    cap = cap_chunks * LANES
    chunks = 3 * cap_chunks
    slab_index = lax.axis_index("slab")
    first = jnp.reshape(slab_index * rows, (1,)).astype(jnp.int32)
    boxed = [x.reshape(lines, LANES) for x in (sensor_rows, sensor_cols, row_frac, col_frac, sensor_weights, owner_order)]
    vmem = pl.BlockSpec(memory_space=VMEM)
    smem = pl.BlockSpec(memory_space=SMEM)
    plan, lo, hi = pl.pallas_call(
        functools.partial(plan_kernel, rows, cap_chunks, blocks),
        out_shape=(
            jax.ShapeDtypeStruct((FIELDS, chunks, LANES), F32),
            jax.ShapeDtypeStruct((keys, LANES), jnp.int32),
            jax.ShapeDtypeStruct((keys, LANES), jnp.int32),
        ),
        in_specs=[smem] + [vmem] * 6,
        out_specs=(vmem, vmem, vmem),
        compiler_params=LIMIT,
        name="plan",
    )(first, *boxed)
    lo = lo[:, 0]
    hi = hi[:, 0]
    value, slots = pl.pallas_call(
        functools.partial(forward_kernel, cap_chunks),
        out_shape=(
            jax.ShapeDtypeStruct((probes, chunks * LANES), F32),
            jax.ShapeDtypeStruct((probes, sensors), F32),
        ),
        in_specs=[vmem, vmem, smem, smem],
        out_specs=(vmem, vmem),
        scratch_shapes=[
            VMEM((depth, BLOCK), BF16),
            VMEM((chunks, depth, LANES), F32),
            VMEM((lines, probes, LANES), F32),
        ],
        compiler_params=LIMIT,
        name="forward",
    )(probe_fields, plan, lo, hi)
    observed = lax.psum_scatter(slots, "slab", scatter_dimension=1, tiled=True)
    down = [(j, (j - 1) % slab_count) for j in range(slab_count)]
    up = [(j, (j + 1) % slab_count) for j in range(slab_count)]
    above = lax.ppermute(value[:, :cap], "slab", down)
    below = lax.ppermute(value[:, 2 * cap :], "slab", up)
    adjoint, trace = pl.pallas_call(
        functools.partial(adjoint_kernel, cap_chunks),
        out_shape=(
            jax.ShapeDtypeStruct((probes, rows, width), BF16),
            jax.ShapeDtypeStruct((1, LANES), F32),
        ),
        in_specs=[vmem, vmem, vmem, vmem, smem, smem],
        out_specs=(vmem, vmem),
        scratch_shapes=[
            VMEM((chunks, depth, LANES), BF16),
            VMEM((depth, BLOCK), F32),
            VMEM((probes, LANES), F32),
        ],
        compiler_params=LIMIT,
        name="adjoint",
    )(value, above, below, plan, lo, hi)
    trace_mean = lax.psum(jnp.sum(trace), ("slab", "probe")) / (probes * probe_groups * sensors)
    return adjoint, observed, trace_mean


def solution(mesh):
    placed = (P("probe", "slab", None), P(), P(), P(), P(), P(), P())
    return jax.shard_map(
        functools.partial(body, mesh.shape["slab"], mesh.shape["probe"]),
        mesh=mesh,
        in_specs=placed,
        out_specs=(P("probe", "slab", None), P("probe", "slab"), P()),
        check_vma=False,
    )
```

time: 343 us -> 143 us (0.42)
  local copies, waits for them, and re-layouts: 161 us -> 4.54 us
  matrix products: 98.4 us -> 0 us
  Pallas kernels: 0 us -> 60 us
  blocking collectives: 12.5 us -> 41.4 us
  waiting for transfers between devices: 34.1 us -> 11.8 us
  other arithmetic: 16.7 us -> 1.34 us
  starting transfers between devices: 0.04 us -> 6.71 us
    gather x5 -> x0, local copies, waits for them, and re-layouts: 115 us -> none  [the longest x1 23 us: body(): owned_colfrac = col_frac[owner_order]]
    dot_general x16 -> x0, matrix products: 98.4 us -> none  [the longest x8 56.2 us: adjoint_block(): piece = jnp.dot(sources, table, preferred_element_type=jnp.float32)]
    pallas_call x0 -> x3, Pallas kernels: none -> 60 us  [the longest x1 28 us: body(): pl.pallas_call(functools.partial(forward_kernel, cap_chunks), out_shape=(...]
    psum x1 -> x0, waiting for transfers between devices: 34.1 us -> none  [body(): observed_all = lax.psum(partial_value, 'slab')]
    psum x1, blocking collectives: 12.5 us -> 41.4 us  [body(): lax.psum(jnp.sum(trace), ('slab', 'probe'))]
    convert_element_type x9 -> x0, local copies, waits for them, and re-layouts: 16.2 us -> none  [the longest x8 16.1 us: body(): (spread[:, None, :] * row_weights[None, :, :]).astype(jnp.bfloat16)]
    reshape x10 -> x0, local copies, waits for them, and re-layouts: 15.2 us -> none  [the longest x1 7.16 us: body(): adjoint_sources = result.reshape(probe_count, row_count, width)]
    ppermute x0 -> x2, waiting for transfers between devices: none -> 11.7 us  [the longest x1 11.7 us: body(): below = lax.ppermute(value[:, 2 * cap:], 'slab', up)]
  transfers between devices with their start and end apart: 1 -> 3, of which waited for: 1 -> 1; matrix products, arithmetic and copies ran while one was open for 7% -> 2% of each run, Pallas kernels for 0% -> 19%
where the time goes in v1:
time: 143 us; the launch traced here: 142 us
  Pallas kernels  60 us (42%)
  blocking collectives  41.4 us (29%)
  between operations  15.8 us (11%)
  waiting for transfers between devices  11.8 us (8%)
  starting transfers between devices  6.71 us (5%)
  local copies, waits for them, and re-layouts  4.54 us (3%)
    psum x1, blocking collectives, body(): lax.psum(jnp.sum(trace), ('slab', 'probe'))  41.4 us
    pallas_call x1, Pallas kernels, body(): pl.pallas_call(functools.partial(forward_kernel, cap_chunks), out_shape=(...  28 us
    pallas_call x1, Pallas kernels, body(): pl.pallas_call(functools.partial(adjoint_kernel, cap_chunks), out_shape=(...  27.4 us
    ppermute x1, waiting for transfers between devices, body(): below = lax.ppermute(value[:, 2 * cap:], 'slab', up)  11.7 us
    ppermute x1, starting transfers between devices, body(): above = lax.ppermute(value[:, :cap], 'slab', down)  6.61 us
    pallas_call x1, Pallas kernels, body(): pl.pallas_call(functools.partial(plan_kernel, rows, cap_chunks, blocks),...  4.59 us
  transfers between devices with their start and end apart: 3, of which 1 were waited for; matrix products, arithmetic and copies ran while one was open for 2% of the time, Pallas kernels for 19%

profile of v1, /device:TPU:4, one launch (start us, length us, event | category | flops | bytes accessed | tf_op | source)
XLA Modules:
  0.0 141.6 jit_solution(14250870082613269187)
XLA Ops:
  7.2 0.0 reduce-scatter.2.cloned.1.call-start
  7.2 4.6 %plan.1 = (f32[11,48,128]{2,1,0:T(8,128)}, s32[192,128]{1,0:T(8,128)}, s32[192,128]{1,0:T(8,128)}) custom-call(s32[1]{0:T(128)} %bitcast.first_ref, s32[32,128]{1,0:T(8,128)} %bitcast.7, s32[32,128]{1,0:T(8,128)} %bitcast.8, f32[32,128]{1,0:T(8,128)} %bitcast.9, f32[32,128]{1,0:T(8,128)} %bitcast.10, f32[32,128]{1,0:T(8,128)} %bitcast.11, s32[32,128]{1,0:T(8,128)} %bitcast.12), custom_call_target="tpu_custom_call" | custom-call | tf_op jit(solution)/shard_map/plan/pallas_call | solution.py:251
  11.8 1.7 %slice_reduce_fusion = (s32[192]{0:T(256)}, s32[192]{0:T(256)}) fusion(s32[192,128]{1,0:T(8,128)} %get-tuple-element.12, s32[192,128]{1,0:T(8,128)} %get-tuple-element.11), kind=kLoop, calls=%fused_computation | loop fusion | bytes 3072 | tf_op jit(solution)/shard_map/slice | solution.py:264
  13.5 28.0 %forward.1 = (f32[64,6144]{1,0:T(8,128)}, f32[64,4096]{1,0:T(8,128)}) custom-call(bf16[64,4,8192]{2,1,0:T(4,128)(2,1)} %field_ref.1, f32[11,48,128]{2,1,0:T(8,128)} %get-tuple-element.10.plan_ref, s32[192]{0:T(256)} %get-tuple-element.20.lo_ref, s32[192]{0:T(256)} %get-tuple-element.19.hi_ref), custom_call_target="tpu_custom_call" | custom-call | tf_op jit(solution)/shard_map/forward/pallas_call | solution.py:265
  41.4 0.0 reduce-scatter.2.cloned.1.call-update
  41.4 1.3 fusion
  42.7 0.1 collective-permute-start.1
  42.8 6.6 %collective-permute-start = (f32[64,2048]{1,0:T(8,128)S(1)}, f32[64,2048]{1,0:T(8,128)S(1)}, u32[]{:S(2)}, u32[]{:S(2)}) collective-permute-start(f32[64,2048]{1,0:T(8,128)S(1)} %get-tuple-element.18), channel_id=1, source_target_pairs={{0,28},{4,0},{8,4},{12,8},{16,12},{20,16},{24,20},{28,24},{1,29},{... | collective-permute-start | bytes 1572872 | tf_op jit(solution)/shard_map/ppermute | solution.py:284
  49.4 11.7 %collective-permute-done.1.below_ref = f32[64,2048]{1,0:T(8,128)S(1)} collective-permute-done((f32[64,2048]{1,0:T(8,128)S(1)}, f32[64,2048]{1,0:T(8,128)S(1)}, u32[]{:S(2)}, u32[]{:S(2)}) %collective-permute-start.1) | collective-permute-done | bytes 524320 | tf_op jit(solution)/shard_map/ppermute | solution.py:285
  61.1 0.0 copy-start
  61.2 0.0 collective-permute-done.above_ref
  61.2 0.8 copy-done
  61.9 0.0 copy-start.1
  61.9 0.8 copy-done.1
  62.8 27.4 %adjoint.1 = (bf16[64,4,8192]{2,1,0:T(4,128)(2,1)}, f32[1,128]{1,0:T(1,128)}) custom-call(f32[64,6144]{1,0:T(8,128)} %get-tuple-element.13.value_ref, f32[64,2048]{1,0:T(8,128)} %copy-done.1, f32[64,2048]{1,0:T(8,128)} %copy-done, f32[11,48,128]{2,1,0:T(8,128)} %get-tuple-element.10.plan_ref, s32[192]{0:T(256)} %get-tuple-element.20.lo_ref, ...), custom_call_target="tpu_custom_call" | custom-call | tf_op jit(solution)/shard_map/adjoint/pallas_call | solution.py:286
  90.2 1.3 reduce_sum.9
  91.5 41.4 %psum.7 = f32[]{:T(128)} all-reduce(f32[]{:T(128)} %reduce_sum.9), channel_id=1, replica_groups=mesh['slab'=8,'probe'=4] {'slab','probe'}, use_global_device_ids=true, to_apply=%region_2.0 | all-reduce | flops 1 | bytes 8 | tf_op jit(solution)/shard_map/psum | solution.py:302
  133.6 0.0 reduce-scatter.2.cloned.1.call-done
Async XLA Ops:
  7.2 126.4 %reduce-scatter.2.cloned.1.call-start = ((), (), s32[]{:S(2)}) async-start(), calls=%async_computation.1 | async-start | bytes 1179648 | tf_op jit(solution)/shard_map/reduce_scatter | solution.py:281
  42.7 18.4 %collective-permute-start.1 = (f32[64,2048]{1,0:T(8,128)S(1)}, f32[64,2048]{1,0:T(8,128)S(1)}, u32[]{:S(2)}, u32[]{:S(2)}) collective-permute-start(f32[64,2048]{1,0:T(8,128)S(1)} %get-tuple-element.17), channel_id=1, source_target_pairs={{0,4},{4,8},{8,12},{12,16},{16,20},{20,24},{24,28},{28,0},{1,5},{5... | collective-permute-start | bytes 1572872 | tf_op jit(solution)/shard_map/ppermute | solution.py:285
  42.8 18.3 %collective-permute-start = (f32[64,2048]{1,0:T(8,128)S(1)}, f32[64,2048]{1,0:T(8,128)S(1)}, u32[]{:S(2)}, u32[]{:S(2)}) collective-permute-start(f32[64,2048]{1,0:T(8,128)S(1)} %get-tuple-element.18), channel_id=1, source_target_pairs={{0,28},{4,0},{8,4},{12,8},{16,12},{20,16},{24,20},{28,24},{1,29},{... | collective-permute-start | bytes 1572872 | tf_op jit(solution)/shard_map/ppermute | solution.py:284
  61.1 0.8 copy-start
  61.9 0.8 copy-start.1
Sparse Core Ops, SparseCore 0:
  41.6 41.4 reduce-scatter.1

commit v2 on v1

v2 whole, which is shorter than its diff:
```python
import functools

import jax
import jax.numpy as jnp
from jax import lax
from jax.experimental import pallas as pl
from jax.experimental.pallas import tpu as pltpu
from jax.sharding import PartitionSpec as P

LANES = 128
BLOCK = 512
HALF = 256
FIELDS = 11
F32 = jnp.float32
BF16 = jnp.bfloat16
NT = (((1,), (1,)), ((), ()))
VMEM = pltpu.VMEM
SMEM = pltpu.SMEM
LIMIT = pltpu.CompilerParams(vmem_limit_bytes=60 * 1024 * 1024)


def iota(shape, dim):
    return lax.broadcasted_iota(jnp.int32, shape, dim)


def nt_dot(a, b):
    return lax.dot_general(a, b, NT, preferred_element_type=F32)


def plan_kernel(rows, cap_chunks, blocks, slabs, pair_lines, me_ref, r_ref, c_ref, rf_ref, cf_ref, w_ref, order_ref, plan_ref, marks_ref, places_ref):
    lines = r_ref.shape[0]
    sensors = lines * LANES
    step = min(4, lines)
    me = me_ref[0]
    first = me * rows
    owned = lines * LANES // slabs
    keys_group = 2 * blocks
    keys = 3 * keys_group
    chunks = 3 * cap_chunks

    def wide(x, i):
        return jnp.concatenate([x[i + j : i + j + 1, :] for j in range(step)], axis=1)

    order = order_ref[...]
    slot = iota((lines, LANES), 0) * LANES + iota((lines, LANES), 1)
    found = jnp.zeros((2 * lines, LANES), F32)
    for i in range(0, lines, step):
        target = wide(order, i)
        mine = wide(slot, i)
        here = iota((lines, step * LANES), 0) == (target >> 7)
        stack = jnp.concatenate(
            [jnp.where(here, (mine >> 7).astype(F32), 0.0), jnp.where(here, (mine & 127).astype(F32), 0.0)], axis=0
        ).astype(BF16)
        place = jnp.where(iota((LANES, step * LANES), 0) == (target & 127), 1.0, 0.0).astype(BF16)
        found = found + nt_dot(stack, place)
    slot_hi = found[:lines, :]
    slot_lo = found[lines:, :]

    r = r_ref[...]
    c = c_ref[...]
    rel = r - first + 1
    valid = (rel >= 0) & (rel <= rows)
    group = jnp.where(rel == 0, 0, jnp.where(rel == rows, 2, 1))
    block = c // BLOCK
    inner = c - block * BLOCK
    half = c // HALF
    slot_of = (slot_hi * LANES + slot_lo).astype(jnp.int32)
    owner = slot_of // owned
    home = r // rows
    send_key = jnp.where(home == me, owner, -1)
    recv_key = jnp.where(owner == me, home, -1)
    key = group * keys_group + 2 * block + jnp.where(inner == BLOCK - 1, 1, 0)
    key = jnp.where(valid, key, -1)

    count = jnp.zeros((keys, 1), F32)
    for i in range(lines):
        count = count + jnp.sum(jnp.where(iota((keys, LANES), 0) == key[i : i + 1, :], 1.0, 0.0), axis=1, keepdims=True)
    big = jnp.floor(count * (1.0 / 64.0))
    small = count - 64.0 * big
    ka, kb = iota((keys, keys), 0), iota((keys, keys), 1)
    below = jnp.where((kb < ka) & (kb // keys_group == ka // keys_group), 1.0, 0.0).astype(BF16)
    start = 64.0 * jnp.dot(below, jnp.broadcast_to(big, (keys, LANES)).astype(BF16), preferred_element_type=F32)
    start = start + jnp.dot(below, jnp.broadcast_to(small, (keys, LANES)).astype(BF16), preferred_element_type=F32)
    start = start + ((iota((keys, LANES), 0) // keys_group) * (cap_chunks * LANES)).astype(F32)
    marks_ref[0] = start.astype(jnp.int32)
    marks_ref[1] = (start + count).astype(jnp.int32)

    upper = jnp.where(iota((LANES, LANES), 0) < iota((LANES, LANES), 1), 1.0, 0.0).astype(BF16)
    carry = jnp.concatenate([start[:, :1], jnp.zeros((2 * slabs, 1), F32)], axis=0)
    spots, sends, recvs = [], [], []
    for i in range(lines):
        hot = jnp.concatenate(
            [
                jnp.where(iota((keys, LANES), 0) == key[i : i + 1, :], 1.0, 0.0),
                jnp.where(iota((slabs, LANES), 0) == send_key[i : i + 1, :], 1.0, 0.0),
                jnp.where(iota((slabs, LANES), 0) == recv_key[i : i + 1, :], 1.0, 0.0),
            ],
            axis=0,
        )
        before = jnp.dot(hot.astype(BF16), upper, preferred_element_type=F32)
        ranks = hot * (before + carry)
        spots.append(jnp.sum(ranks[:keys], axis=0, keepdims=True))
        sends.append(jnp.sum(ranks[keys : keys + slabs], axis=0, keepdims=True))
        recvs.append(jnp.sum(ranks[keys + slabs :], axis=0, keepdims=True))
        carry = carry + jnp.sum(hot, axis=1, keepdims=True)
    spot = jnp.concatenate(spots, axis=0).astype(jnp.int32)
    spot = jnp.where(valid, spot, -1)
    send = jnp.concatenate(sends, axis=0).astype(jnp.int32)
    recv = jnp.concatenate(recvs, axis=0).astype(jnp.int32)
    send_line = jnp.where(send_key >= 0, owner * pair_lines + (send >> 7), 200)
    recv_line = jnp.where(recv_key >= 0, home * pair_lines + (recv >> 7), -1)

    rf = rf_ref[...]
    cf = cf_ref[...]
    w = w_ref[...]
    rf_top = rf.astype(BF16).astype(F32)
    w_top = w.astype(BF16).astype(F32)
    values = [
        half.astype(F32),
        (c - half * HALF).astype(F32),
        (1.0 - cf).astype(BF16).astype(F32),
        cf.astype(BF16).astype(F32),
        rf_top,
        rf - rf_top,
        w_top,
        w - w_top,
        rel.astype(F32),
        send_line.astype(F32),
        (send & 127).astype(F32),
    ]
    total = jnp.zeros((FIELDS * chunks, LANES), F32)
    for i in range(0, lines, step):
        target = wide(spot, i)
        here = iota((chunks, step * LANES), 0) == (target >> 7)
        stack = jnp.concatenate([jnp.where(here, wide(v, i), 0.0) for v in values], axis=0).astype(BF16)
        place = jnp.where(iota((LANES, step * LANES), 0) == (target & 127), 1.0, 0.0).astype(BF16)
        total = total + nt_dot(stack, place)
    for f in range(FIELDS):
        plan_ref[f] = total[f * chunks : (f + 1) * chunks, :]

    slot_here = slot_of - me * owned
    received = slabs * pair_lines
    found = jnp.zeros((2 * received, LANES), F32)
    for i in range(0, lines, step):
        here = iota((received, step * LANES), 0) == wide(recv_line, i)
        target = wide(slot_here, i)
        stack = jnp.concatenate(
            [jnp.where(here, (target >> 7).astype(F32), 0.0), jnp.where(here, (target & 127).astype(F32), 0.0)], axis=0
        ).astype(BF16)
        place = jnp.where(iota((LANES, step * LANES), 0) == (wide(recv, i) & 127), 1.0, 0.0).astype(BF16)
        found = found + nt_dot(stack, place)
    places_ref[...] = (found[:received] * LANES + found[received:]).astype(jnp.int32)


def column_table(plan_ref, chunk, number):
    line = pl.ds(chunk, 1)
    column = (plan_ref[0, line, :] * HALF + plan_ref[1, line, :]).astype(jnp.int32) - number * BLOCK
    cells = iota((BLOCK, LANES), 0)
    return jnp.where(
        cells == column, plan_ref[2, line, :], jnp.where(cells == column + 1, plan_ref[3, line, :], 0.0)
    ).astype(BF16)


def row_pattern(plan_ref, chunk, rows, depth):
    line = pl.ds(chunk, 1)
    rf = plan_ref[4, line, :] + plan_ref[5, line, :]
    rel = plan_ref[8, line, :].astype(jnp.int32)
    row = iota((depth, LANES), 0) % rows + 1
    return jnp.where(row == rel, 1.0 - rf, jnp.where(row == rel + 1, rf, 0.0))


def group_chunks(marks_ref, group, keys_group, base):
    return (marks_ref[1, (group + 1) * keys_group - 1, 0] - base + LANES - 1) // LANES


def chunk_range(marks_ref, group, number, keys_group):
    at = group * keys_group + 2 * number
    begin = marks_ref[0, jnp.maximum(at - 1, group * keys_group), 0]
    end = marks_ref[1, at + 1, 0]
    return begin // LANES, jnp.where(end > begin, (end + LANES - 1) // LANES, begin // LANES)


def forward_kernel(cap_chunks, field_ref, plan_ref, marks_ref, value_ref, flat, sums):
    probes, rows, width = field_ref.shape
    depth = probes * rows
    blocks = width // BLOCK
    keys_group = 2 * blocks
    counts = [group_chunks(marks_ref, g, keys_group, g * cap_chunks * LANES) for g in range(3)]
    for g in range(3):

        @pl.loop(0, counts[g])
        def _(k):
            sums[g * cap_chunks + k] = jnp.zeros((depth, LANES), F32)

    @pl.loop(0, blocks)
    def _(number):
        cols = pl.ds(pl.multiple_of(number * BLOCK, BLOCK), BLOCK)
        flat[...] = field_ref[:, :, cols].astype(F32).reshape(depth, BLOCK).astype(BF16)
        for g in range(3):
            begin, end = chunk_range(marks_ref, g, number, keys_group)

            @pl.loop(begin, end)
            def _(chunk):
                table = column_table(plan_ref, chunk, number)
                sums[chunk] += jnp.dot(flat[...], table, preferred_element_type=F32)

    fold = jnp.where(iota((probes, depth), 1) // rows == iota((probes, depth), 0), 1.0, 0.0).astype(BF16)
    for g in range(3):

        @pl.loop(0, counts[g])
        def _(k):
            chunk = g * cap_chunks + k
            scaled = (sums[chunk] * row_pattern(plan_ref, chunk, rows, depth)).astype(BF16)
            value_ref[:, pl.ds(pl.multiple_of(chunk * LANES, LANES), LANES)] = jnp.dot(
                fold, scaled, preferred_element_type=F32
            )


def merge_kernel(cap_chunks, blocks, value_ref, above_ref, below_ref, plan_ref, marks_ref, spread_ref, packed_ref, trace_ref, squares):
    outgoing, probes, _ = packed_ref.shape
    keys_group = 2 * blocks
    squares[...] = jnp.zeros_like(squares)
    packed_ref[...] = jnp.zeros_like(packed_ref)
    for g in range(3):
        count = group_chunks(marks_ref, g, keys_group, g * cap_chunks * LANES)

        @pl.loop(0, count)
        def _(k):
            chunk = g * cap_chunks + k
            value = value_ref[:, pl.ds(pl.multiple_of(chunk * LANES, LANES), LANES)]
            near = pl.ds(pl.multiple_of(k * LANES, LANES), LANES)
            if g == 0:
                value = value + below_ref[:, near]
            if g == 2:
                value = value + above_ref[:, near]
            line = pl.ds(chunk, 1)
            spread = value * (plan_ref[6, line, :] + plan_ref[7, line, :])
            spread_ref[chunk] = spread.astype(BF16)
            if g > 0:
                squares[...] += spread * value
                high = plan_ref[9, line, :].astype(jnp.int32)
                low = plan_ref[10, line, :].astype(jnp.int32)
                place = jnp.where(iota((LANES, LANES), 0) == low, 1.0, 0.0).astype(BF16)
                stack = jnp.concatenate([jnp.where(high == d, value, 0.0) for d in range(outgoing)], axis=0).astype(BF16)
                packed_ref[...] += nt_dot(stack, place).reshape(outgoing, probes, LANES)

    trace_ref[...] = jnp.sum(squares[...], axis=0, keepdims=True)


def unpack_kernel(packed_ref, places_ref, observed_ref):
    received, probes, _ = packed_ref.shape
    owned = observed_ref.shape[1]
    total = jnp.zeros((probes, owned), F32)
    for d in range(received):
        place = jnp.where(iota((owned, LANES), 0) == places_ref[d : d + 1, :], 1.0, 0.0).astype(BF16)
        total = total + nt_dot(packed_ref[d].astype(BF16), place)
    observed_ref[...] = total


def adjoint_kernel(cap_chunks, spread_ref, plan_ref, marks_ref, out_ref, sources, total):
    probes, rows, width = out_ref.shape
    depth = probes * rows
    blocks = width // BLOCK
    keys_group = 2 * blocks
    raise_rows = jnp.where(iota((depth, probes), 0) // rows == iota((depth, probes), 1), 1.0, 0.0).astype(BF16)
    for g in range(3):
        count = group_chunks(marks_ref, g, keys_group, g * cap_chunks * LANES)

        @pl.loop(0, count)
        def _(k):
            chunk = g * cap_chunks + k
            raised = jnp.dot(raise_rows, spread_ref[chunk], preferred_element_type=F32)
            sources[chunk] = (raised * row_pattern(plan_ref, chunk, rows, depth)).astype(BF16)

    @pl.loop(0, blocks)
    def _(number):
        total[...] = jnp.zeros_like(total)
        for g in range(3):
            begin, end = chunk_range(marks_ref, g, number, keys_group)

            @pl.loop(begin, end)
            def _(chunk):
                total[...] += nt_dot(sources[chunk], column_table(plan_ref, chunk, number))

        cols = pl.ds(pl.multiple_of(number * BLOCK, BLOCK), BLOCK)
        out_ref[:, :, cols] = total[...].reshape(probes, rows, BLOCK).astype(BF16)


def body(slab_count, probe_groups, probe_fields, sensor_rows, sensor_cols, row_frac, col_frac, sensor_weights, owner_order):
    probes, rows, width = probe_fields.shape
    sensors = sensor_rows.shape[0]
    depth = probes * rows
    lines = sensors // LANES
    blocks = width // BLOCK
    keys = 6 * blocks
    most = min(sensors, 4 * sensors // slab_count)
    cap_chunks = -(-most // (8 * LANES)) * 8
    cap = cap_chunks * LANES
    chunks = 3 * cap_chunks
    pair_lines = -(-most // (slab_count * LANES))
    outgoing = slab_count * pair_lines
    me = jnp.reshape(lax.axis_index("slab"), (1,)).astype(jnp.int32)
    boxed = [x.reshape(lines, LANES) for x in (sensor_rows, sensor_cols, row_frac, col_frac, sensor_weights, owner_order)]
    vmem = pl.BlockSpec(memory_space=VMEM)
    smem = pl.BlockSpec(memory_space=SMEM)
    plan, marks, places = pl.pallas_call(
        functools.partial(plan_kernel, rows, cap_chunks, blocks, slab_count, pair_lines),
        out_shape=(
            jax.ShapeDtypeStruct((FIELDS, chunks, LANES), F32),
            jax.ShapeDtypeStruct((2, keys, LANES), jnp.int32),
            jax.ShapeDtypeStruct((outgoing, LANES), jnp.int32),
        ),
        in_specs=[smem] + [vmem] * 6,
        out_specs=(vmem, vmem, vmem),
        compiler_params=LIMIT,
        name="plan",
    )(me, *boxed)
    value = pl.pallas_call(
        functools.partial(forward_kernel, cap_chunks),
        out_shape=jax.ShapeDtypeStruct((probes, chunks * LANES), F32),
        in_specs=[vmem, vmem, smem],
        out_specs=vmem,
        scratch_shapes=[
            VMEM((depth, BLOCK), BF16),
            VMEM((chunks, depth, LANES), F32),
        ],
        compiler_params=LIMIT,
        name="forward",
    )(probe_fields, plan, marks)
    down = [(j, (j - 1) % slab_count) for j in range(slab_count)]
    up = [(j, (j + 1) % slab_count) for j in range(slab_count)]
    above = lax.ppermute(value[:, :cap], "slab", down)
    below = lax.ppermute(value[:, 2 * cap :], "slab", up)
    spread, packed, trace = pl.pallas_call(
        functools.partial(merge_kernel, cap_chunks, blocks),
        out_shape=(
            jax.ShapeDtypeStruct((chunks, probes, LANES), BF16),
            jax.ShapeDtypeStruct((outgoing, probes, LANES), F32),
            jax.ShapeDtypeStruct((1, LANES), F32),
        ),
        in_specs=[vmem, vmem, vmem, vmem, smem],
        out_specs=(vmem, vmem, vmem),
        scratch_shapes=[VMEM((probes, LANES), F32)],
        compiler_params=LIMIT,
        name="merge",
    )(value, above, below, plan, marks)
    arrived = lax.all_to_all(packed, "slab", 0, 0, tiled=True)
    adjoint = pl.pallas_call(
        functools.partial(adjoint_kernel, cap_chunks),
        out_shape=jax.ShapeDtypeStruct((probes, rows, width), BF16),
        in_specs=[vmem, vmem, smem],
        out_specs=vmem,
        scratch_shapes=[
            VMEM((chunks, depth, LANES), BF16),
            VMEM((depth, BLOCK), F32),
        ],
        compiler_params=LIMIT,
        cost_estimate=pl.CostEstimate(flops=4 * 10**9, bytes_accessed=8 * 10**6, transcendentals=0),
        name="adjoint",
    )(spread, plan, marks)
    observed = pl.pallas_call(
        unpack_kernel,
        out_shape=jax.ShapeDtypeStruct((probes, sensors // slab_count), F32),
        in_specs=[vmem, vmem],
        out_specs=vmem,
        compiler_params=LIMIT,
        name="unpack",
    )(arrived, places)
    trace_mean = lax.psum(jnp.sum(trace), ("slab", "probe")) / (probes * probe_groups * sensors)
    return adjoint, observed, trace_mean


def solution(mesh):
    placed = (P("probe", "slab", None), P(), P(), P(), P(), P(), P())
    return jax.shard_map(
        functools.partial(body, mesh.shape["slab"], mesh.shape["probe"]),
        mesh=mesh,
        in_specs=placed,
        out_specs=(P("probe", "slab", None), P("probe", "slab"), P()),
        check_vma=False,
    )
```

time: 143 us -> 126 us (0.88); the launches traced: 142 us -> 127 us
  between operations: 15.8 us -> 2.45 us
  waiting for transfers between devices: 11.8 us -> 7.41 us
  Pallas kernels: 60 us -> 63.4 us
    ppermute x1, waiting for transfers between devices: 11.7 us -> 7.4 us  [body(): below = lax.ppermute(value[:, 2 * cap:], 'slab', up)]
    ppermute x1, starting transfers between devices: 6.61 us -> 2.63 us  [body(): above = lax.ppermute(value[:, :cap], 'slab', down)]
    all_to_all x0 -> x1, starting transfers between devices: none -> 3.44 us  [body(): arrived = lax.all_to_all(packed, 'slab', 0, 0, tiled=True)]
    pallas_call x3 -> x5, Pallas kernels: 60 us -> 63.4 us  [the longest x1 25.2 us: body(): pl.pallas_call(functools.partial(adjoint_kernel, cap_chunks), out_shape=j...]
    slice x1 -> x0, local copies, waits for them, and re-layouts: 1.65 us -> none  [body(): hi = hi[:, 0]]
  transfers between devices with their start and end apart: 3 -> 3, of which waited for: 1 -> 1; matrix products, arithmetic and copies ran while one was open for 2% -> 1% of each run, Pallas kernels for 19% -> 20%
where the time goes in v2:
time: 126 us; the launch traced here: 127 us
  Pallas kernels  63.4 us (50%)
  blocking collectives  42.2 us (33%)
  waiting for transfers between devices  7.41 us (6%)
  starting transfers between devices  6.13 us (5%)
  local copies, waits for them, and re-layouts  3.72 us (3%)
  between operations  2.45 us (2%)
  other arithmetic  1.26 us (1%)
    psum x1, blocking collectives, body(): lax.psum(jnp.sum(trace), ('slab', 'probe'))  42.2 us
    pallas_call x1, Pallas kernels, body(): pl.pallas_call(functools.partial(adjoint_kernel, cap_chunks), out_shape=j...  25.2 us
    pallas_call x1, Pallas kernels, body(): pl.pallas_call(functools.partial(forward_kernel, cap_chunks), out_shape=j...  23.7 us
    pallas_call x1, Pallas kernels, body(): pl.pallas_call(functools.partial(merge_kernel, cap_chunks, blocks), out_s...  7.49 us
    ppermute x1, waiting for transfers between devices, body(): below = lax.ppermute(value[:, 2 * cap:], 'slab', up)  7.4 us
    pallas_call x1, Pallas kernels, body(): pl.pallas_call(functools.partial(plan_kernel, rows, cap_chunks, blocks, s...  4.53 us
    all_to_all x1, starting transfers between devices, body(): arrived = lax.all_to_all(packed, 'slab', 0, 0, tiled=True)  3.44 us
    ppermute x1, starting transfers between devices, body(): above = lax.ppermute(value[:, :cap], 'slab', down)  2.63 us
  transfers between devices with their start and end apart: 3, of which 1 were waited for; matrix products, arithmetic and copies ran while one was open for 1% of the time, Pallas kernels for 20%

profile of v2, /device:TPU:4, one launch (start us, length us, event | category | flops | bytes accessed | tf_op | source)
XLA Modules:
  0.0 126.5 jit_solution(16188283704196864590)
XLA Ops:
  0.6 4.5 %plan.1 = (f32[11,48,128]{2,1,0:T(8,128)}, s32[2,96,128]{2,1,0:T(8,128)}, s32[16,128]{1,0:T(8,128)}) custom-call(s32[1]{0:T(128)} %bitcast.me_ref, s32[32,128]{1,0:T(8,128)} %bitcast.7, s32[32,128]{1,0:T(8,128)} %bitcast.8, f32[32,128]{1,0:T(8,128)} %bitcast.9, f32[32,128]{1,0:T(8,128)} %bitcast.10, f32[32,128]{1,0:T(8,128)} %bitcast.11, s32[32,128]{1,0:T(8,128)} %bitcast.12), custom_call_target="tpu_custom_call" | custom-call | tf_op jit(solution)/shard_map/plan/pallas_call | solution.py:306
  5.2 23.7 %forward.1.value_ref = f32[64,6144]{1,0:T(8,128)} custom-call(bf16[64,4,8192]{2,1,0:T(4,128)(2,1)} %field_ref.1, f32[11,48,128]{2,1,0:T(8,128)} %get-tuple-element.9.plan_ref, s32[2,96,128]{2,1,0:T(8,128)} %get-tuple-element.10.marks_ref), custom_call_target="tpu_custom_call" | custom-call | tf_op jit(solution)/shard_map/forward/pallas_call | solution.py:318
  28.9 1.3 %fusion = (f32[64,2048]{1,0:T(8,128)S(1)}, f32[64,2048]{1,0:T(8,128)S(1)}) fusion(f32[64,6144]{1,0:T(8,128)} %forward.1.value_ref), kind=kLoop, calls=%fused_computation | loop fusion | bytes 2097152 | tf_op jit(solution)/shard_map/slice | solution.py:333
  30.2 0.1 collective-permute-start.1
  30.2 2.6 %collective-permute-start = (f32[64,2048]{1,0:T(8,128)S(1)}, f32[64,2048]{1,0:T(8,128)S(1)}, u32[]{:S(2)}, u32[]{:S(2)}) collective-permute-start(f32[64,2048]{1,0:T(8,128)S(1)} %get-tuple-element.16), channel_id=1, source_target_pairs={{0,28},{4,0},{8,4},{12,8},{16,12},{20,16},{24,20},{28,24},{1,29},{... | collective-permute-start | bytes 1572872 | tf_op jit(solution)/shard_map/ppermute | solution.py:332
  32.9 7.4 %collective-permute-done.1.below_ref = f32[64,2048]{1,0:T(8,128)S(1)} collective-permute-done((f32[64,2048]{1,0:T(8,128)S(1)}, f32[64,2048]{1,0:T(8,128)S(1)}, u32[]{:S(2)}, u32[]{:S(2)}) %collective-permute-start.1) | collective-permute-done | bytes 524320 | tf_op jit(solution)/shard_map/ppermute | solution.py:333
  40.3 0.0 copy-start.1
  40.3 0.0 collective-permute-done.above_ref
  40.3 0.8 copy-done.1
  41.1 0.0 copy-start.2
  41.1 0.8 copy-done.2
  41.9 7.5 %merge.1 = (bf16[48,64,128]{2,1,0:T(8,128)(2,1)}, f32[16,64,128]{2,1,0:T(8,128)}, f32[1,128]{1,0:T(1,128)}) custom-call(f32[64,6144]{1,0:T(8,128)} %forward.1.value_ref, f32[64,2048]{1,0:T(8,128)} %copy-done.2, f32[64,2048]{1,0:T(8,128)} %copy-done.1, f32[11,48,128]{2,1,0:T(8,128)} %get-tuple-element.9.plan_ref, s32[2,96,128]{2,1,0:T(8,128)} %get-tuple-element.10.marks_ref), custom_call_target="tpu_custom_call" | custom-call | tf_op jit(solution)/shard_map/merge/pallas_call | solution.py:334
  49.4 3.4 %all-to-all-start = ((f32[16,64,128]{2,1,0:T(8,128)}), f32[16,64,128]{2,1,0:T(8,128)S(1)}, u32[]{:S(2)}, u32[]{:S(2)}) async-start(f32[16,64,128]{2,1,0:T(8,128)} %get-tuple-element.12), calls=%async_computation | async-start | bytes 1048576 | tf_op jit(solution)/shard_map/all_to_all | solution.py:347
  52.8 1.3 reduce_sum.9
  54.1 42.2 %psum.7 = f32[]{:T(128)} all-reduce(f32[]{:T(128)} %reduce_sum.9), channel_id=1, replica_groups=mesh['slab'=8,'probe'=4] {'slab','probe'}, use_global_device_ids=true, to_apply=%region_1.0 | all-reduce | flops 1 | bytes 8 | tf_op jit(solution)/shard_map/psum | solution.py:369
  96.9 25.2 %adjoint.1 = bf16[64,4,8192]{2,1,0:T(4,128)(2,1)} custom-call(bf16[48,64,128]{2,1,0:T(8,128)(2,1)} %get-tuple-element.11.spread_ref, f32[11,48,128]{2,1,0:T(8,128)} %get-tuple-element.9.plan_ref, s32[2,96,128]{2,1,0:T(8,128)} %get-tuple-element.10.marks_ref), custom_call_target="tpu_custom_call" | custom-call | flops 4000000000 | bytes 8000000 | tf_op jit(solution)/shard_map/adjoint/pallas_call | solution.py:348
  122.1 0.0 all-to-all-done.packed_ref
  122.1 0.0 copy-start
  122.1 0.8 copy-done
  122.9 2.5 %unpack.1 = f32[64,512]{1,0:T(8,128)} custom-call(f32[16,64,128]{2,1,0:T(8,128)} %copy-done, s32[16,128]{1,0:T(8,128)} %get-tuple-element.13.places_ref), custom_call_target="tpu_custom_call" | custom-call | tf_op jit(solution)/shard_map/unpack/pallas_call | solution.py:361
Async XLA Ops:
  30.2 10.1 %collective-permute-start.1 = (f32[64,2048]{1,0:T(8,128)S(1)}, f32[64,2048]{1,0:T(8,128)S(1)}, u32[]{:S(2)}, u32[]{:S(2)}) collective-permute-start(f32[64,2048]{1,0:T(8,128)S(1)} %get-tuple-element.15), channel_id=1, source_target_pairs={{0,4},{4,8},{8,12},{12,16},{16,20},{20,24},{24,28},{28,0},{1,5},{5... | collective-permute-start | bytes 1572872 | tf_op jit(solution)/shard_map/ppermute | solution.py:333
  30.2 10.0 %collective-permute-start = (f32[64,2048]{1,0:T(8,128)S(1)}, f32[64,2048]{1,0:T(8,128)S(1)}, u32[]{:S(2)}, u32[]{:S(2)}) collective-permute-start(f32[64,2048]{1,0:T(8,128)S(1)} %get-tuple-element.16), channel_id=1, source_target_pairs={{0,28},{4,0},{8,4},{12,8},{16,12},{20,16},{24,20},{28,24},{1,29},{... | collective-permute-start | bytes 1572872 | tf_op jit(solution)/shard_map/ppermute | solution.py:332
  40.3 0.8 copy-start.1
  41.1 0.8 copy-start.2
  49.4 72.7 %all-to-all-start = ((f32[16,64,128]{2,1,0:T(8,128)}), f32[16,64,128]{2,1,0:T(8,128)S(1)}, u32[]{:S(2)}, u32[]{:S(2)}) async-start(f32[16,64,128]{2,1,0:T(8,128)} %get-tuple-element.12), calls=%async_computation | async-start | bytes 1048576 | tf_op jit(solution)/shard_map/all_to_all | solution.py:347
  122.1 0.8 copy-start
